TPU v7x, 128 devices: a whole 4x4x4 slice. The times are simulated.
128 devices in a mesh: dp: 16 (over x, z), blk: 8 (over y, core).
Axes of the slice: x: 4, y: 4, z: 4, core: 2. Of those that a mesh axis runs over, the one named last changes fastest.
Arguments:
- entity_table: float32 [262144, 400], P(('dp', 'blk')), may hold values from -1.8 to 1.8
- adagrad_sum: float32 [262144], P(('dp', 'blk')), may hold values from 0.0001 to 0.001
- relations: float32 [7424, 400], replicated, may hold values from -1.8 to 1.8
- owner_map: int32 [262144], replicated, may hold values from 0 to 262143, as said below
- head_ids: int32 [16384], P(('dp', 'blk')), may hold values from 0 to 262143, as said below
- rel_ids: int32 [16384], P(('dp', 'blk')), may hold values from 0 to 7423
- tail_ids: int32 [16384], P(('dp', 'blk')), may hold values from 0 to 262143, as said below
- neg_ids: int32 [65536], P(('dp', 'blk')), may hold values from 0 to 262143, as said below
Outputs:
- new_table: float32 [262144, 400], P(('dp', 'blk'))
- new_sum: float32 [262144], P(('dp', 'blk'))
Inputs may be any that keep to these rules, and one draw needn't show every extreme that they name: `owner_map`: A permutation: every storage position appears once. The owner of position p is device p // 2048. `head_ids`: among the 128 heads, 128 tails and 512 negatives of one device taken together, at most 12 are stored on any one owner; in every draw 16 owners receive exactly 12 from every device. `tail_ids`: counted together with the heads and negatives of the same device, as stated for head_ids. `neg_ids`: counted together with the heads and tails of the same device, as stated for head_ids.
All inputs are finite; a program needn't handle non-finite values.
Results may differ from a plain program's by a relative error of at most 0.00005.
Values sent between devices are 32-bit elements; how exact they have to be, the bound alone decides.
A program may use at most 128 MiB of HBM per device.

v0:
```python
import jax
import jax.numpy as jnp
from jax import lax
from jax.sharding import PartitionSpec as P

MARGIN = 10.0
EPSILON = 1e-05
LEARNING_RATE = 0.1


def negative_terms(queries, neg_block, weight):
    query_sq = jnp.sum(queries * queries, axis=1)
    block_sq = jnp.sum(neg_block * neg_block, axis=1)
    inner_prod = jnp.dot(
        queries, neg_block.T, precision=lax.Precision.HIGHEST, preferred_element_type=jnp.float32
    )
    distance = jnp.sqrt(query_sq[:, None] + block_sq[None, :] - 2.0 * inner_prod + EPSILON)
    coefficient = -jax.nn.sigmoid(MARGIN - distance) / (weight * distance)
    grad_query = queries * jnp.sum(coefficient, axis=1)[:, None] - jnp.dot(
        coefficient, neg_block, precision=lax.Precision.HIGHEST, preferred_element_type=jnp.float32
    )
    grad_block = neg_block * jnp.sum(coefficient, axis=0)[:, None] - jnp.dot(
        coefficient.T, queries, precision=lax.Precision.HIGHEST, preferred_element_type=jnp.float32
    )
    return (grad_query, grad_block)


def send_requests(requests):
    return lax.all_to_all(requests, ("dp", "blk"), split_axis=0, concat_axis=0, tiled=True)


def move_rows(payload):
    return lax.all_to_all(payload, ("dp", "blk"), split_axis=0, concat_axis=0, tiled=True)


def on_device(
    entity_table, adagrad_sum, relations, owner_map, head_ids, rel_ids, tail_ids, neg_ids
):
    dp_count = lax.axis_size("dp")
    blk_count = lax.axis_size("blk")
    owner_count = dp_count * blk_count
    rows_here, width = entity_table.shape
    edge_count = head_ids.shape[0]
    neg_count = neg_ids.shape[0]
    request_count = 2 * edge_count + neg_count
    capacity = max(2, 2 * request_count // owner_count)
    wanted = jnp.concatenate([head_ids, tail_ids, neg_ids])
    position = owner_map[wanted]
    owner_of = position // rows_here
    local_row = position % rows_here
    onehot = (owner_of[:, None] == jnp.arange(owner_count, dtype=jnp.int32)[None, :]).astype(
        jnp.int32
    )
    before = jnp.cumsum(onehot, axis=0) - onehot
    rank_in = jnp.sum(before * onehot, axis=1)
    slot_of = owner_of * capacity + rank_in
    requests = jnp.zeros((owner_count * capacity,), jnp.int32).at[slot_of].set(local_row)
    requests = requests.reshape(owner_count, capacity)
    asked_rows = send_requests(requests)
    served = entity_table[asked_rows]
    fetched = move_rows(served).reshape(owner_count * capacity, width)[slot_of]
    head_rows = fetched[:edge_count]
    tail_rows = fetched[edge_count : 2 * edge_count]
    neg_block = fetched[2 * edge_count :]
    queries = head_rows + relations[rel_ids]
    residue = queries - tail_rows
    pos_dist = jnp.sqrt(jnp.sum(residue * residue, axis=1) + EPSILON)
    grad_pos = (jax.nn.sigmoid(pos_dist - MARGIN) / pos_dist)[:, None] * residue
    weight = float(blk_count * neg_count)
    part_query, part_block = negative_terms(
        queries, lax.all_gather(neg_block, "blk", axis=0, tiled=True), weight
    )
    block_grad = lax.psum_scatter(part_block, "blk", scatter_dimension=0, tiled=True)
    gradients = jnp.concatenate([grad_pos + part_query, -grad_pos, block_grad])
    outgoing = jnp.zeros((owner_count * capacity, width), jnp.float32).at[slot_of].set(gradients)
    incoming = move_rows(outgoing.reshape(owner_count, capacity, width))
    summed = (
        jnp.zeros_like(entity_table).at[asked_rows.reshape(-1)].add(incoming.reshape(-1, width))
    )
    new_sum = adagrad_sum + jnp.mean(summed * summed, axis=1)
    new_table = entity_table - LEARNING_RATE * summed / jnp.sqrt(new_sum)[:, None]
    return (new_table, new_sum)


def solution(mesh):
    return jax.shard_map(
        on_device,
        mesh=mesh,
        in_specs=(
            P(("dp", "blk"), None),
            P(("dp", "blk")),
            P(),
            P(),
            P(("dp", "blk")),
            P(("dp", "blk")),
            P(("dp", "blk")),
            P(("dp", "blk")),
        ),
        out_specs=(P(("dp", "blk"), None), P(("dp", "blk"))),
        check_vma=False,
    )
```

profile of v0, /device:TPU:1, one launch (start us, length us, event | category | flops | bytes accessed | tf_op | source)
XLA Modules:
  0.0 335.3 jit_solution(6407851075444210870)
XLA Ops:
  7.2 0.8 fusion.20
  8.0 0.4 copy-done
  8.4 4.5 %gather_fusion = s32[768]{0:T(1024)S(1)} fusion(s32[262144]{0:T(1024)S(1)} %copy-done, s32[1024]{0:T(1024)S(1)} %pad_clamp_fusion.3), kind=kCustom, calls=%fused_computation | custom fusion | bytes 9216 | tf_op jit(solution)/shard_map/gather | solution.py:48
  12.9 0.1 copy.29
  13.1 0.2 fusion.8
  13.4 0.3 fusion.11
  13.8 3.4 %scatter_custom_fusion = s32[1536]{0:T(1024)S(1)} fusion(s32[768]{0:T(1024)S(1)} %fusion.21, s32[768]{0:T(1024)S(1)} %get-tuple-element.15, s32[]{:T(128)} %constant.22.clone.1), kind=kCustom, calls=%fused_computation.64 | custom fusion | bytes 6148 | tf_op jit(solution)/shard_map/scatter | solution.py:57
  17.2 0.7 all_to_all.14
  17.9 11.5 %all-to-all-start = ((s32[128,1,12]{2,1,0:T(1,128)}), s32[128,1,12]{2,1,0:T(1,128)S(1)}, u32[]{:S(2)}, u32[]{:S(2)}) async-start(s32[128,1,12]{2,1,0:T(1,128)} %bitcast.7), calls=%async_computation | async-start | bytes 131072 | tf_op jit(solution)/shard_map/all_to_all | solution.py:29
  29.4 5.1 %copy.39 = f32[2048,400]{1,0:T(8,128)} copy(f32[2048,400]{0,1:T(8,128)} %param.8) | data formatting | bytes 6553600 | tf_op args[0]
  34.4 4.4 %all-to-all-done = s32[128,1,12]{2,1,0:T(1,128)S(1)} async-done(((s32[128,1,12]{2,1,0:T(1,128)}), s32[128,1,12]{2,1,0:T(1,128)S(1)}, u32[]{:S(2)}, u32[]{:S(2)}) %all-to-all-start) | async-done | bytes 6176 | tf_op jit(solution)/shard_map/all_to_all | solution.py:29
  38.8 0.1 reshape.314
  38.9 7.9 %gather_fusion.1 = f32[1536,400]{1,0:T(8,128)} fusion(f32[2048,400]{1,0:T(8,128)} %copy.39, s32[2048]{0:T(1024)S(1)} %pad_clamp_fusion), kind=kCustom, calls=%fused_computation.1 | custom fusion | bytes 4921344 | tf_op jit(solution)/shard_map/gather | solution.py:60
  46.8 4.6 %reshape.313 = f32[128,12,400]{2,1,0:T(8,128)} reshape(f32[1536,400]{1,0:T(8,128)} %gather_fusion.1) | data formatting | bytes 4915200 | tf_op jit(solution)/shard_map/gather | solution.py:60
  51.4 5.9 %all-to-all-start.1 = ((f32[128,12,400]{2,1,0:T(8,128)}), f32[128,12,400]{2,1,0:T(8,128)}, u32[]{:S(2)}, u32[]{:S(2)}) async-start(f32[128,12,400]{2,1,0:T(8,128)} %reshape.313), calls=%async_computation.1 | async-start | bytes 8388608 | tf_op jit(solution)/shard_map/all_to_all | solution.py:33
  57.3 52.5 %all-to-all-done.1 = f32[128,12,400]{2,1,0:T(8,128)} async-done(((f32[128,12,400]{2,1,0:T(8,128)}), f32[128,12,400]{2,1,0:T(8,128)}, u32[]{:S(2)}, u32[]{:S(2)}) %all-to-all-start.1) | async-done | bytes 2457632 | tf_op jit(solution)/shard_map/all_to_all | solution.py:33
  109.8 4.6 %reshape.301 = f32[1536,400]{1,0:T(8,128)} reshape(f32[128,12,400]{2,1,0:T(8,128)} %all-to-all-done.1) | data formatting | bytes 4915200 | tf_op jit(solution)/shard_map/reshape | solution.py:61
  114.4 4.7 %gather_fusion.2 = f32[768,400]{1,0:T(8,128)S(1)} fusion(f32[1536,400]{1,0:T(8,128)} %reshape.301, s32[1024]{0:T(1024)S(1)} %pad_clamp_fusion.2), kind=kCustom, calls=%fused_computation.2 | custom fusion | bytes 2460672 | tf_op jit(solution)/shard_map/gather | solution.py:61
  119.1 1.2 copy.43
  120.4 0.2 reduce-scatter.2.cloned.1.call-start
  120.6 14.2 %copy.34 = f32[7424,400]{1,0:T(8,128)} copy(f32[7424,400]{0,1:T(8,128)} %param.10) | data formatting | bytes 23756800 | tf_op args[2]
  134.8 6.5 %gather_fusion.3 = f32[128,400]{1,0:T(8,128)S(1)} fusion(f32[7424,400]{1,0:T(8,128)} %copy.34, s32[1024]{0:T(1024)S(1)} %pad_clamp_fusion.1), kind=kCustom, calls=%fused_computation.3 | custom fusion | bytes 410112 | tf_op jit(solution)/shard_map/gather | solution.py:65
  141.3 0.1 copy.35
  141.5 0.1 copy.41
  141.6 0.1 copy.42
  141.9 18.3 %all-gather.2.cloned.1.call-done = f32[4096,400]{0,1:T(8,128)} async-done(((f32[512,400]{0,1:T(8,128)}), f32[4096,400]{0,1:T(8,128)}) %all-gather.2.cloned.1.call-update) | async-done | bytes 6553616 | tf_op jit(solution)/shard_map/all_gather | solution.py:71
  160.3 3.6 %multiply_reduce_fusion = f32[4096]{0:T(1024)S(1)} fusion(f32[4096,400]{0,1:T(8,128)} %all-gather.2.cloned.1.call-done), kind=kLoop, calls=%fused_computation.8 | loop fusion | flops 3272704 | bytes 6569984 | tf_op jit(solution)/shard_map/reduce_sum | solution.py:13
  163.9 1.1 copy-done.3
  165.0 5.5 %fusion.23 = (f32[128]{0:T(128)S(1)}, f32[4096]{0:T(1024)S(1)}, f32[128,4096]{1,0:T(8,128)S(1)}) fusion(f32[128,400]{0,1:T(8,128)S(1)} %get-tuple-element.12, f32[4096,400]{0,1:T(8,128)S(1)} %copy-done.3, f32[4096]{0:T(1024)S(1)} %multiply_reduce_fusion, f32[128]{0:T(128)S(1)} %multiply_reduce_fusion.2), kind=kOutput, calls=%fused_computation.73 | convolution fusion | flops 2523394048 | bytes 8889344 | tf_op jit(solution)/shard_map/dot_general | solution.py:14
  170.5 7.6 %multiply_subtract_fusion = f32[4096,400]{0,1:T(8,128)} fusion(f32[4096,400]{0,1:T(8,128)S(1)} %copy-done.3, f32[128,4096]{1,0:T(8,128)S(1)} %get-tuple-element.17, f32[128,400]{0,1:T(8,128)S(1)} %get-tuple-element.12, f32[4096]{0:T(1024)S(1)} %get-tuple-element.7), kind=kOutput, calls=%fused_computation.7 | convolution fusion | flops 2519859200 | bytes 15425536 | tf_op jit(solution)/shard_map/dot_general | solution.py:22
  178.2 7.6 %fusion.7 = f32[128,400]{0,1:T(8,128)S(1)} fusion(f32[128,4096]{1,0:T(8,128)S(1)} %get-tuple-element.17, f32[4096,400]{0,1:T(8,128)} %all-gather.2.cloned.1.call-done, f32[128,400]{0,1:T(8,128)S(1)} %get-tuple-element.12, f32[128,400]{0,1:T(8,128)S(1)} %get-tuple-element.11, f32[128]{0:T(128)S(1)} %get-tuple-element.6, f32[128]{0:T(128)S(1)} %multiply_divide_fusion.1), kind=kOutput, calls=%fused_computation.22 | convolution fusion | flops 2516787200 | bytes 9266176 | tf_op jit(solution)/shard_map/dot_general | solution.py:19
  185.8 35.3 %reduce-scatter.2.cloned.1.call-done = f32[512,400]{0,1:T(8,128)} async-done(((f32[4096,400]{0,1:T(8,128)}), f32[512,400]{0,1:T(8,128)}) %reduce-scatter.2.cloned.1.call-update) | async-done | bytes 819216 | tf_op jit(solution)/shard_map/reduce_scatter | solution.py:73
  221.1 1.2 pad_maximum_fusion
  222.3 1.6 copy.38
  223.9 8.0 %scatter_custom_fusion.1 = f32[1536,400]{1,0:T(8,128)} fusion(s32[768]{0:T(1024)S(1)} %fusion.21, f32[768,400]{1,0:T(8,128)} %copy.38, f32[]{:T(128)} %constant.21.clone.1), kind=kCustom, calls=%fused_computation.18 | custom fusion | bytes 2458112 | tf_op jit(solution)/shard_map/scatter | solution.py:75
  232.0 4.6 %reshape.302 = f32[128,12,400]{2,1,0:T(8,128)} reshape(f32[1536,400]{1,0:T(8,128)} %scatter_custom_fusion.1) | data formatting | bytes 4915200 | tf_op jit(solution)/shard_map/reshape | solution.py:76
  236.5 8.9 %all-to-all-start.2 = ((f32[128,12,400]{2,1,0:T(8,128)}), f32[128,12,400]{2,1,0:T(8,128)}, u32[]{:S(2)}, u32[]{:S(2)}) async-start(f32[128,12,400]{2,1,0:T(8,128)} %reshape.302), calls=%async_computation.3 | async-start | bytes 8388608 | tf_op jit(solution)/shard_map/all_to_all | solution.py:33
  245.4 0.5 broadcast.247
  245.9 0.8 reduce.9
  246.7 0.1 reshape.300
  246.9 51.1 %all-to-all-done.2 = f32[128,12,400]{2,1,0:T(8,128)} async-done(((f32[128,12,400]{2,1,0:T(8,128)}), f32[128,12,400]{2,1,0:T(8,128)}, u32[]{:S(2)}, u32[]{:S(2)}) %all-to-all-start.2) | async-done | bytes 2457632 | tf_op jit(solution)/shard_map/all_to_all | solution.py:33
  297.9 4.6 %reshape.356 = f32[1536,400]{1,0:T(8,128)} reshape(f32[128,12,400]{2,1,0:T(8,128)} %all-to-all-done.2) | data formatting | bytes 4915200 | tf_op jit(solution)/shard_map/reshape | solution.py:78
  302.5 12.4 %scatter_custom_fusion.2 = f32[2048,400]{1,0:T(8,128)} fusion(s32[1536]{0:T(1024)S(1)} %fusion.13, f32[1536,400]{1,0:T(8,128)} %reshape.356, f32[]{:T(128)} %constant.21.clone.1), kind=kCustom, calls=%fused_computation.16 | custom fusion | flops 614400 | bytes 3277312 | tf_op jit(solution)/shard_map/scatter-add | solution.py:78
  314.9 2.7 multiply_reduce_fusion.1
  317.6 0.6 fusion.24
  318.2 0.1 copy-done.2
  318.4 4.9 %divide_subtract_fusion = f32[2048,400]{1,0:T(8,128)} fusion(f32[2048,400]{1,0:T(8,128)S(1)} %copy-done.2, f32[2048,400]{1,0:T(8,128)} %scatter_custom_fusion.2, f32[2048]{0:T(1024)S(1)} %get-tuple-element.8), kind=kLoop, calls=%fused_computation.13 | loop fusion | flops 2457600 | bytes 9838592 | tf_op jit(solution)/shard_map/sub | solution.py:81
  323.3 5.2 %copy.40 = f32[2048,400]{0,1:T(8,128)} copy(f32[2048,400]{1,0:T(8,128)} %divide_subtract_fusion) | data formatting | bytes 6553600
  (32 shorter events, 0.7 us)
Async XLA Ops:
  7.2 1.3 copy-start
  17.9 20.9 %all-to-all-start = ((s32[128,1,12]{2,1,0:T(1,128)}), s32[128,1,12]{2,1,0:T(1,128)S(1)}, u32[]{:S(2)}, u32[]{:S(2)}) async-start(s32[128,1,12]{2,1,0:T(1,128)} %bitcast.7), calls=%async_computation | async-start | bytes 131072 | tf_op jit(solution)/shard_map/all_to_all | solution.py:29
  51.4 58.4 %all-to-all-start.1 = ((f32[128,12,400]{2,1,0:T(8,128)}), f32[128,12,400]{2,1,0:T(8,128)}, u32[]{:S(2)}, u32[]{:S(2)}) async-start(f32[128,12,400]{2,1,0:T(8,128)} %reshape.313), calls=%async_computation.1 | async-start | bytes 8388608 | tf_op jit(solution)/shard_map/all_to_all | solution.py:33
  57.2 103.0 %all-gather.2.cloned.1.call-start = ((), (), s32[]{:S(2)}) async-start(), calls=%async_computation.4 | async-start | bytes 7372800 | tf_op jit(solution)/shard_map/all_gather | solution.py:71
  120.3 14.5 %copy-start.5 = (s32[128]{0:T(128)S(1)}, s32[128]{0:T(128)}, u32[]{:S(2)}) copy-start(s32[128]{0:T(128)} %param.13) | copy-start | bytes 1540
  120.4 100.7 %reduce-scatter.2.cloned.1.call-start = ((), (), s32[]{:S(2)}) async-start(), calls=%async_computation.5 | async-start | bytes 7372800 | tf_op jit(solution)/shard_map/reduce_scatter | solution.py:73
  160.2 4.7 %copy-start.3 = (f32[4096,400]{0,1:T(8,128)S(1)}, f32[4096,400]{0,1:T(8,128)}, u32[]{:S(2)}) copy-start(f32[4096,400]{0,1:T(8,128)} %all-gather.2.cloned.1.call-done) | copy-start | bytes 19660804
  236.5 61.4 %all-to-all-start.2 = ((f32[128,12,400]{2,1,0:T(8,128)}), f32[128,12,400]{2,1,0:T(8,128)}, u32[]{:S(2)}, u32[]{:S(2)}) async-start(f32[128,12,400]{2,1,0:T(8,128)} %reshape.302), calls=%async_computation.3 | async-start | bytes 8388608 | tf_op jit(solution)/shard_map/all_to_all | solution.py:33
  314.9 2.7 copy-start.4
  314.9 3.5 %copy-start.2 = (f32[2048,400]{1,0:T(8,128)S(1)}, f32[2048,400]{1,0:T(8,128)}, u32[]{:S(2)}) copy-start(f32[2048,400]{1,0:T(8,128)} %copy.39) | copy-start | bytes 9830404
  318.4 10.1 %copy-start.1 = (s32[262144]{0:T(1024)S(1)}, s32[262144]{0:T(1024)}, u32[]{:S(2)}) copy-start(s32[262144]{0:T(1024)} %param.11) | copy-start | bytes 3145732
Sparse Core Ops, SparseCore 0:
  120.5 39.7 all-gather.1
  178.3 42.7 reduce-scatter.1
where the time goes:
time: 337 us; the launch traced here: 335 us
  waiting for transfers between devices  162 us (48%)
  local copies, waits for them, and re-layouts  84.3 us (25%)
  other arithmetic  28 us (8%)
  starting transfers between devices  26.5 us (8%)
  matrix products  20.8 us (6%)
  between operations  14.3 us (4%)
    all_to_all x2, waiting for transfers between devices, move_rows(): lax.all_to_all(payload, ('dp', 'blk'), split_axis=0, concat_axis=0, tiled...  104 us
    reduce_scatter x1, waiting for transfers between devices, on_device(): lax.psum_scatter(part_block, 'blk', scatter_dimension=0, tiled=True)  35.3 us
    unnamed x18, local copies, waits for them, and re-layouts  27.6 us
    all_gather x1, waiting for transfers between devices, on_device(): lax.all_gather(neg_block, 'blk', axis=0, tiled=True)  18.3 us
    all_to_all x2, starting transfers between devices, move_rows(): lax.all_to_all(payload, ('dp', 'blk'), split_axis=0, concat_axis=0, tiled...  14.7 us
    gather x2, local copies, waits for them, and re-layouts, on_device(): served = entity_table[asked_rows]  12.4 us
    scatter-add x1, other arithmetic, on_device(): jnp.zeros_like(entity_table).at[asked_rows.reshape(-1)]  12.4 us
    all_to_all x1, starting transfers between devices, send_requests(): lax.all_to_all(requests, ('dp', 'blk'), split_axis=0, concat_axis=0, tile...  11.5 us
  transfers between devices with their start and end apart: 5, of which 5 were waited for; matrix products, arithmetic and copies ran while one was open for 11% of the time, Pallas kernels for 0%

commit v1 on v0

--- a/solution.py
+++ b/solution.py
@@ -67,9 +67,10 @@
     pos_dist = jnp.sqrt(jnp.sum(residue * residue, axis=1) + EPSILON)
     grad_pos = (jax.nn.sigmoid(pos_dist - MARGIN) / pos_dist)[:, None] * residue
     weight = float(blk_count * neg_count)
-    part_query, part_block = negative_terms(
-        queries, lax.all_gather(neg_block, "blk", axis=0, tiled=True), weight
+    obtain_ports_now = lambda load, dev_axis: jnp.concatenate(
+        lax.all_to_all(jnp.stack([load] * lax.axis_size(dev_axis)), dev_axis, 0, 0), axis=0
     )
+    part_query, part_block = negative_terms(queries, obtain_ports_now(neg_block, "blk"), weight)
     block_grad = lax.psum_scatter(part_block, "blk", scatter_dimension=0, tiled=True)
     gradients = jnp.concatenate([grad_pos + part_query, -grad_pos, block_grad])
     outgoing = jnp.zeros((owner_count * capacity, width), jnp.float32).at[slot_of].set(gradients)

time: 337 us -> 381 us (1.13)
  waiting for transfers between devices: 162 us -> 193 us
  starting transfers between devices: 26.5 us -> 32.1 us
  local copies, waits for them, and re-layouts: 84.3 us -> 89.1 us
    all_to_all x0 -> x1, waiting for transfers between devices: none -> 53.3 us  [on_device(): lax.all_to_all(jnp.stack([load] * lax.axis_size(dev_axis)), dev_axis, 0, 0)]
    all_gather x1 -> x0, waiting for transfers between devices: 18.3 us -> none  [on_device(): lax.all_gather(neg_block, 'blk', axis=0, tiled=True)]
    all_to_all x0 -> x1, starting transfers between devices: none -> 5.91 us  [on_device(): lax.all_to_all(jnp.stack([load] * lax.axis_size(dev_axis)), dev_axis, 0, 0)]
  transfers between devices with their start and end apart: 5 -> 5, of which waited for: 5 -> 5; matrix products, arithmetic and copies ran while one was open for 11% -> 9% of each run, Pallas kernels for 0% -> 0%
where the time goes in v1:
time: 381 us; the launch traced here: 380 us
  waiting for transfers between devices  193 us (51%)
  local copies, waits for them, and re-layouts  89.1 us (23%)
  starting transfers between devices  32.1 us (8%)
  other arithmetic  30.4 us (8%)
  matrix products  20.8 us (5%)
  between operations  14.3 us (4%)
    all_to_all x2, waiting for transfers between devices, move_rows(): lax.all_to_all(payload, ('dp', 'blk'), split_axis=0, concat_axis=0, tiled...  104 us
    all_to_all x1, waiting for transfers between devices, on_device(): lax.all_to_all(jnp.stack([load] * lax.axis_size(dev_axis)), dev_axis, 0, 0)  53.3 us
    reduce_scatter x1, waiting for transfers between devices, on_device(): lax.psum_scatter(part_block, 'blk', scatter_dimension=0, tiled=True)  32.1 us
    unnamed x18, local copies, waits for them, and re-layouts  25.1 us
    all_to_all x2, starting transfers between devices, move_rows(): lax.all_to_all(payload, ('dp', 'blk'), split_axis=0, concat_axis=0, tiled...  14.6 us
    gather x2, local copies, waits for them, and re-layouts, on_device(): served = entity_table[asked_rows]  12.4 us
    scatter-add x1, other arithmetic, on_device(): jnp.zeros_like(entity_table).at[asked_rows.reshape(-1)]  12.4 us
    all_to_all x1, starting transfers between devices, send_requests(): lax.all_to_all(requests, ('dp', 'blk'), split_axis=0, concat_axis=0, tile...  11.5 us
  transfers between devices with their start and end apart: 5, of which 5 were waited for; matrix products, arithmetic and copies ran while one was open for 9% of the time, Pallas kernels for 0%

profile of v1, /device:TPU:1, one launch (start us, length us, event | category | flops | bytes accessed | tf_op | source)
XLA Modules:
  0.0 380.0 jit_solution(3929962567320525594)
XLA Ops:
  7.2 0.8 fusion.20
  8.0 0.4 copy-done
  8.4 4.5 %gather_fusion = s32[768]{0:T(1024)S(1)} fusion(s32[262144]{0:T(1024)S(1)} %copy-done, s32[1024]{0:T(1024)S(1)} %pad_clamp_fusion.3), kind=kCustom, calls=%fused_computation | custom fusion | bytes 9216 | tf_op jit(solution)/shard_map/gather | solution.py:48
  12.9 0.1 copy.29
  13.1 0.2 fusion.8
  13.4 0.3 fusion.11
  13.8 3.4 scatter_custom_fusion
  17.2 0.7 all_to_all.17
  17.9 11.5 %all-to-all-start = ((s32[128,1,12]{2,1,0:T(1,128)}), s32[128,1,12]{2,1,0:T(1,128)S(1)}, u32[]{:S(2)}, u32[]{:S(2)}) async-start(s32[128,1,12]{2,1,0:T(1,128)} %bitcast.7), calls=%async_computation | async-start | bytes 131072 | tf_op jit(solution)/shard_map/all_to_all | solution.py:29
  29.4 5.0 %copy.40 = f32[2048,400]{1,0:T(8,128)} copy(f32[2048,400]{0,1:T(8,128)} %param.8) | data formatting | bytes 6553600 | tf_op args[0]
  34.4 4.4 %all-to-all-done = s32[128,1,12]{2,1,0:T(1,128)S(1)} async-done(((s32[128,1,12]{2,1,0:T(1,128)}), s32[128,1,12]{2,1,0:T(1,128)S(1)}, u32[]{:S(2)}, u32[]{:S(2)}) %all-to-all-start) | async-done | bytes 6176 | tf_op jit(solution)/shard_map/all_to_all | solution.py:29
  38.9 7.9 %gather_fusion.1 = f32[1536,400]{1,0:T(8,128)} fusion(f32[2048,400]{1,0:T(8,128)} %copy.40, s32[2048]{0:T(1024)S(1)} %pad_clamp_fusion), kind=kCustom, calls=%fused_computation.1 | custom fusion | bytes 4921344 | tf_op jit(solution)/shard_map/gather | solution.py:60
  46.8 4.6 %reshape.321 = f32[128,12,400]{2,1,0:T(8,128)} reshape(f32[1536,400]{1,0:T(8,128)} %gather_fusion.1) | data formatting | bytes 4915200 | tf_op jit(solution)/shard_map/gather | solution.py:60
  51.4 5.8 %all-to-all-start.1 = ((f32[128,12,400]{2,1,0:T(8,128)}), f32[128,12,400]{2,1,0:T(8,128)}, u32[]{:S(2)}, u32[]{:S(2)}) async-start(f32[128,12,400]{2,1,0:T(8,128)} %reshape.321), calls=%async_computation.1 | async-start | bytes 8388608 | tf_op jit(solution)/shard_map/all_to_all | solution.py:33
  57.2 52.5 %all-to-all-done.1 = f32[128,12,400]{2,1,0:T(8,128)} async-done(((f32[128,12,400]{2,1,0:T(8,128)}), f32[128,12,400]{2,1,0:T(8,128)}, u32[]{:S(2)}, u32[]{:S(2)}) %all-to-all-start.1) | async-done | bytes 2457632 | tf_op jit(solution)/shard_map/all_to_all | solution.py:33
  109.7 4.6 %reshape.308 = f32[1536,400]{1,0:T(8,128)} reshape(f32[128,12,400]{2,1,0:T(8,128)} %all-to-all-done.1) | data formatting | bytes 4915200 | tf_op jit(solution)/shard_map/reshape | solution.py:61
  114.3 4.7 %gather_fusion.2 = f32[768,400]{1,0:T(8,128)S(1)} fusion(f32[1536,400]{1,0:T(8,128)} %reshape.308, s32[1024]{0:T(1024)S(1)} %pad_clamp_fusion.2), kind=kCustom, calls=%fused_computation.2 | custom fusion | bytes 2460672 | tf_op jit(solution)/shard_map/gather | solution.py:61
  119.1 0.3 copy.37
  119.4 3.6 stack.2
  123.0 5.9 %all-to-all-start.2 = ((f32[8,512,400]{1,2,0:T(8,128)}), f32[8,512,400]{1,2,0:T(8,128)}, u32[]{:S(2)}, u32[]{:S(2)}) async-start(f32[8,512,400]{1,2,0:T(8,128)} %stack.2), calls=%async_computation.2 | async-start | bytes 13107200 | tf_op jit(solution)/shard_map/all_to_all | solution.py:71
  128.9 14.1 %copy.34 = f32[7424,400]{1,0:T(8,128)} copy(f32[7424,400]{0,1:T(8,128)} %param.10) | data formatting | bytes 23756800 | tf_op args[2]
  143.1 6.2 %gather_fusion.3 = f32[128,400]{1,0:T(8,128)S(1)} fusion(f32[7424,400]{1,0:T(8,128)} %copy.34, s32[1024]{0:T(1024)S(1)} %pad_clamp_fusion.1), kind=kCustom, calls=%fused_computation.3 | custom fusion | bytes 410112 | tf_op jit(solution)/shard_map/gather | solution.py:65
  149.3 0.1 copy.35
  149.4 0.1 copy.42
  149.6 0.1 copy.43
  149.8 53.3 %all-to-all-done.2 = f32[8,512,400]{1,2,0:T(8,128)} async-done(((f32[8,512,400]{1,2,0:T(8,128)}), f32[8,512,400]{1,2,0:T(8,128)}, u32[]{:S(2)}, u32[]{:S(2)}) %all-to-all-start.2) | async-done | bytes 6553632 | tf_op jit(solution)/shard_map/all_to_all | solution.py:71
  203.1 3.6 copy.44
  206.8 6.1 %multiply_reduce_fusion = f32[8,512]{1,0:T(8,128)S(1)} fusion(f32[8,512,400]{1,2,0:T(8,128)} %all-to-all-done.2), kind=kLoop, calls=%fused_computation.8 | loop fusion | flops 3272704 | bytes 6569984 | tf_op jit(solution)/shard_map/reduce_sum | solution.py:13
  212.9 5.5 %fusion.23 = (f32[128]{0:T(128)S(1)}, f32[4096]{0:T(1024)S(1)}, f32[128,4096]{1,0:T(8,128)S(1)}) fusion(f32[128,400]{0,1:T(8,128)S(1)} %get-tuple-element.12, f32[4096,400]{0,1:T(8,128)S(1)} %bitcast.44, f32[4096]{0:T(1024)S(1)} %bitcast.50, f32[128]{0:T(128)S(1)} %multiply_reduce_fusion.2), kind=kOutput, calls=%fused_computation.73 | convolution fusion | flops 2523394048 | bytes 8889344 | tf_op jit(solution)/shard_map/dot_general | solution.py:14
  218.4 7.6 %multiply_subtract_fusion = f32[4096,400]{0,1:T(8,128)} fusion(f32[4096,400]{0,1:T(8,128)S(1)} %bitcast.45, f32[128,4096]{1,0:T(8,128)S(1)} %get-tuple-element.17, f32[128,400]{0,1:T(8,128)S(1)} %get-tuple-element.12, f32[4096]{0:T(1024)S(1)} %get-tuple-element.7), kind=kOutput, calls=%fused_computation.7 | convolution fusion | flops 2519859200 | bytes 15425536 | tf_op jit(solution)/shard_map/dot_general | solution.py:22
  226.1 7.6 %fusion.7 = f32[128,400]{0,1:T(8,128)S(1)} fusion(f32[128,4096]{1,0:T(8,128)S(1)} %get-tuple-element.17, f32[4096,400]{0,1:T(8,128)} %bitcast.46, f32[128,400]{0,1:T(8,128)S(1)} %get-tuple-element.12, f32[128,400]{0,1:T(8,128)S(1)} %get-tuple-element.11, f32[128]{0:T(128)S(1)} %get-tuple-element.6, f32[128]{0:T(128)S(1)} %multiply_divide_fusion.1), kind=kOutput, calls=%fused_computation.22 | convolution fusion | flops 2516787200 | bytes 9266176 | tf_op jit(solution)/shard_map/dot_general | solution.py:19
  233.7 32.1 %reduce-scatter.2.cloned.1.call-done = f32[512,400]{0,1:T(8,128)} async-done(((f32[4096,400]{0,1:T(8,128)}), f32[512,400]{0,1:T(8,128)}) %reduce-scatter.2.cloned.1.call-update) | async-done | bytes 819216 | tf_op jit(solution)/shard_map/reduce_scatter | solution.py:74
  265.8 1.2 pad_maximum_fusion
  267.0 1.6 copy.39
  268.7 8.0 %scatter_custom_fusion.1 = f32[1536,400]{1,0:T(8,128)} fusion(s32[768]{0:T(1024)S(1)} %fusion.21, f32[768,400]{1,0:T(8,128)} %copy.39, f32[]{:T(128)} %constant.21.clone.1), kind=kCustom, calls=%fused_computation.18 | custom fusion | bytes 2458112 | tf_op jit(solution)/shard_map/scatter | solution.py:76
  276.7 4.6 %reshape.310 = f32[128,12,400]{2,1,0:T(8,128)} reshape(f32[1536,400]{1,0:T(8,128)} %scatter_custom_fusion.1) | data formatting | bytes 4915200 | tf_op jit(solution)/shard_map/reshape | solution.py:77
  281.2 8.9 %all-to-all-start.3 = ((f32[128,12,400]{2,1,0:T(8,128)}), f32[128,12,400]{2,1,0:T(8,128)}, u32[]{:S(2)}, u32[]{:S(2)}) async-start(f32[128,12,400]{2,1,0:T(8,128)} %reshape.310), calls=%async_computation.4 | async-start | bytes 8388608 | tf_op jit(solution)/shard_map/all_to_all | solution.py:33
  290.1 0.5 broadcast.248
  290.6 0.8 reduce.10
  291.4 0.1 reshape.307
  291.6 51.1 %all-to-all-done.3 = f32[128,12,400]{2,1,0:T(8,128)} async-done(((f32[128,12,400]{2,1,0:T(8,128)}), f32[128,12,400]{2,1,0:T(8,128)}, u32[]{:S(2)}, u32[]{:S(2)}) %all-to-all-start.3) | async-done | bytes 2457632 | tf_op jit(solution)/shard_map/all_to_all | solution.py:33
  342.6 4.6 %reshape.364 = f32[1536,400]{1,0:T(8,128)} reshape(f32[128,12,400]{2,1,0:T(8,128)} %all-to-all-done.3) | data formatting | bytes 4915200 | tf_op jit(solution)/shard_map/reshape | solution.py:79
  347.2 12.4 %scatter_custom_fusion.2 = f32[2048,400]{1,0:T(8,128)} fusion(s32[1536]{0:T(1024)S(1)} %fusion.13, f32[1536,400]{1,0:T(8,128)} %reshape.364, f32[]{:T(128)} %constant.21.clone.1), kind=kCustom, calls=%fused_computation.16 | custom fusion | flops 614400 | bytes 3277312 | tf_op jit(solution)/shard_map/scatter-add | solution.py:79
  359.6 2.7 multiply_reduce_fusion.1
  362.3 0.6 fusion.24
  362.9 0.1 copy-done.2
  363.1 4.9 %divide_subtract_fusion = f32[2048,400]{1,0:T(8,128)} fusion(f32[2048,400]{1,0:T(8,128)S(1)} %copy-done.2, f32[2048,400]{1,0:T(8,128)} %scatter_custom_fusion.2, f32[2048]{0:T(1024)S(1)} %get-tuple-element.8), kind=kLoop, calls=%fused_computation.13 | loop fusion | flops 2457600 | bytes 9838592 | tf_op jit(solution)/shard_map/sub | solution.py:82
  368.0 5.2 %copy.41 = f32[2048,400]{0,1:T(8,128)} copy(f32[2048,400]{1,0:T(8,128)} %divide_subtract_fusion) | data formatting | bytes 6553600
  (34 shorter events, 0.7 us)
Async XLA Ops:
  7.2 1.3 copy-start
  17.9 20.9 %all-to-all-start = ((s32[128,1,12]{2,1,0:T(1,128)}), s32[128,1,12]{2,1,0:T(1,128)S(1)}, u32[]{:S(2)}, u32[]{:S(2)}) async-start(s32[128,1,12]{2,1,0:T(1,128)} %bitcast.7), calls=%async_computation | async-start | bytes 131072 | tf_op jit(solution)/shard_map/all_to_all | solution.py:29
  51.4 58.3 %all-to-all-start.1 = ((f32[128,12,400]{2,1,0:T(8,128)}), f32[128,12,400]{2,1,0:T(8,128)}, u32[]{:S(2)}, u32[]{:S(2)}) async-start(f32[128,12,400]{2,1,0:T(8,128)} %reshape.321), calls=%async_computation.1 | async-start | bytes 8388608 | tf_op jit(solution)/shard_map/all_to_all | solution.py:33
  123.0 80.1 %all-to-all-start.2 = ((f32[8,512,400]{1,2,0:T(8,128)}), f32[8,512,400]{1,2,0:T(8,128)}, u32[]{:S(2)}, u32[]{:S(2)}) async-start(f32[8,512,400]{1,2,0:T(8,128)} %stack.2), calls=%async_computation.2 | async-start | bytes 13107200 | tf_op jit(solution)/shard_map/all_to_all | solution.py:71
  128.9 14.1 %copy-start.5 = (s32[128]{0:T(128)S(1)}, s32[128]{0:T(128)}, u32[]{:S(2)}) copy-start(s32[128]{0:T(128)} %param.13) | copy-start | bytes 1540
  128.9 136.9 %reduce-scatter.2.cloned.1.call-start = ((), (), s32[]{:S(2)}) async-start(), calls=%async_computation.5 | async-start | bytes 7372800 | tf_op jit(solution)/shard_map/reduce_scatter | solution.py:74
  206.8 11.6 %copy-start.3 = (f32[8,50,8,512]{3,2,0,1:T(8,128)}, f32[8,50,8,512]{3,2,0,1:T(8,128)S(1)}, u32[]{:S(2)}) copy-start(f32[8,50,8,512]{3,2,0,1:T(8,128)S(1)} %copy.44) | copy-start | bytes 19660804
  281.2 61.4 %all-to-all-start.3 = ((f32[128,12,400]{2,1,0:T(8,128)}), f32[128,12,400]{2,1,0:T(8,128)}, u32[]{:S(2)}, u32[]{:S(2)}) async-start(f32[128,12,400]{2,1,0:T(8,128)} %reshape.310), calls=%async_computation.4 | async-start | bytes 8388608 | tf_op jit(solution)/shard_map/all_to_all | solution.py:33
  359.6 2.7 copy-start.4
  359.6 3.5 copy-start.2
  363.1 10.1 %copy-start.1 = (s32[262144]{0:T(1024)S(1)}, s32[262144]{0:T(1024)}, u32[]{:S(2)}) copy-start(s32[262144]{0:T(1024)} %param.11) | copy-start | bytes 3145732
Sparse Core Ops, SparseCore 0:
  226.2 39.5 reduce-scatter.1
